TPU v7x, 32 devices: a whole 2x2x4 slice. The times are simulated.
32 devices in a mesh: group: 2 (over x), azim: 16 (over z, y, core).
Axes of the slice: x: 2, y: 2, z: 4, core: 2. Of those that a mesh axis runs over, the one named last changes fastest.
Arguments:
- field: bfloat16 [704, 8, 8, 640], P(('group', 'azim')), parts along dimension 0, may hold values from -6 to 6
- jacobian: bfloat16 [5, 8, 2, 320, 320], P(None, None, None, 'azim'), may hold values from -0.109375 to 0.109375
- coupling: int32 [16, 5], replicated, may hold values 0 or 1
Outputs:
- transferred: bfloat16 [704, 8, 8, 640], P(('group', 'azim')), parts along dimension 0
There are 2 independent parts, one for each index of `group`. A program takes and returns all parts, laid end to end along the dimension named above; an argument that names none is the same for every part. Nothing has to cross between parts.
All inputs are finite; a program needn't handle non-finite values.
Results may differ from a plain program's by a relative error of at most 0.0049.
Values may be sent and summed in bfloat16 or wider, within the bound.
No kernel may reach another device: no remote copies, remote signals or barrier semaphores. Data moves between devices by JAX's collectives and lax.ppermute only.
A program may use at most 128 MiB of HBM per device.

v0:
```python
import math
import jax
import jax.numpy as jnp
import numpy as np
from jax import lax
from jax.sharding import PartitionSpec as P

BLADES = 22


def twiddles(row_count, col_count, modulus):
    rows_iota = jnp.arange(row_count, dtype=jnp.int32)[:, None]
    cols_iota = jnp.arange(col_count, dtype=jnp.int32)[None, :]
    phase = rows_iota * cols_iota % modulus
    angle = phase.astype(jnp.float32) * (2.0 * math.pi / modulus)
    return (jnp.cos(angle), jnp.sin(angle))


def real_form(jac_item):
    jac_real = jac_item[:, 0]
    jac_imag = jac_item[:, 1]
    upper = jnp.concatenate([jac_real, -jac_imag], axis=2)
    lower = jnp.concatenate([jac_imag, jac_real], axis=2)
    return jnp.concatenate([upper, lower], axis=1)


def shards(field, jacobian, coupling):
    local_stations, axial_count, freq_count, full_width = field.shape
    node_count = lax.axis_size("azim")
    item_count = axial_count * freq_count
    per_device = item_count // node_count
    half_width = full_width // 2
    order_count = jacobian.shape[0]
    precise = lax.Precision.HIGH
    flattened = field.reshape(local_stations, item_count, full_width)
    columns = lax.all_to_all(flattened, "azim", split_axis=1, concat_axis=0, tiled=True)
    targets = np.arange(node_count * per_device) % freq_count
    outgoing = jnp.take(jacobian, jnp.asarray(targets, dtype=jnp.int32), axis=1)
    local_jac = lax.all_to_all(outgoing, "azim", split_axis=1, concat_axis=3, tiled=True)
    stations = columns.shape[0]
    passage = stations // BLADES
    norm_scale = 1.0 / math.sqrt(stations)
    cos_blade, sin_blade = twiddles(BLADES, BLADES, BLADES)
    cos_twist, sin_twist = twiddles(BLADES, passage, stations)
    cos_pass, sin_pass = twiddles(passage, passage, passage)
    twist_c = cos_twist[:, :, None]
    twist_s = sin_twist[:, :, None]
    gate_table = coupling.astype(jnp.bfloat16)

    def transform(position, buffer):
        sample = lax.dynamic_index_in_dim(columns, position, 1, keepdims=False)
        values = sample.astype(jnp.float32).reshape(BLADES, passage, full_width)
        first_c = jnp.einsum("rb,bav->rav", cos_blade, values, precision=precise)
        first_s = jnp.einsum("rb,bav->rav", sin_blade, values, precision=precise)
        part_real = first_c[..., :half_width] + first_s[..., half_width:]
        part_imag = first_c[..., half_width:] - first_s[..., :half_width]
        turned = jnp.concatenate(
            [twist_c * part_real + twist_s * part_imag, twist_c * part_imag - twist_s * part_real],
            axis=-1,
        )
        second_c = jnp.einsum("qa,rav->qrv", cos_pass, turned, precision=precise)
        second_s = jnp.einsum("qa,rav->qrv", sin_pass, turned, precision=precise)
        modes = (
            jnp.concatenate(
                [
                    second_c[..., :half_width] + second_s[..., half_width:],
                    second_c[..., half_width:] - second_s[..., :half_width],
                ],
                axis=-1,
            )
            * norm_scale
        ).astype(jnp.bfloat16)
        operator = real_form(lax.dynamic_index_in_dim(local_jac, position, 1, keepdims=False))
        coupled = jnp.zeros((passage, BLADES, full_width), jnp.float32)
        for order_idx in range(order_count):
            moved = (
                jnp.roll(modes, -(order_idx - order_count // 2), axis=0)
                * gate_table[:, order_idx][:, None, None]
            )
            coupled = coupled + jnp.einsum(
                "qri,oi->qro", moved, operator[order_idx], preferred_element_type=jnp.float32
            )
        third_c = jnp.einsum("qa,qrv->rav", cos_pass, coupled, precision=precise)
        third_s = jnp.einsum("qa,qrv->rav", sin_pass, coupled, precision=precise)
        back_real = third_c[..., :half_width] - third_s[..., half_width:]
        back_imag = third_c[..., half_width:] + third_s[..., :half_width]
        spun = jnp.concatenate(
            [twist_c * back_real - twist_s * back_imag, twist_c * back_imag + twist_s * back_real],
            axis=-1,
        )
        last_c = jnp.einsum("rb,rav->bav", cos_blade, spun, precision=precise)
        last_s = jnp.einsum("rb,rav->bav", sin_blade, spun, precision=precise)
        restored = (
            jnp.concatenate(
                [
                    last_c[..., :half_width] - last_s[..., half_width:],
                    last_c[..., half_width:] + last_s[..., :half_width],
                ],
                axis=-1,
            )
            * norm_scale
        )
        result = restored.reshape(stations, full_width).astype(jnp.bfloat16)
        return lax.dynamic_update_index_in_dim(buffer, result, position, 1)

    initial = jnp.zeros((stations, per_device, full_width), jnp.bfloat16)
    finished = lax.fori_loop(0, per_device, transform, initial)
    returned = lax.all_to_all(finished, "azim", split_axis=0, concat_axis=1, tiled=True)
    return returned.reshape(local_stations, axial_count, freq_count, full_width)


def solution(mesh):
    placed = (P(("group", "azim"), None, None, None), P(None, None, None, "azim", None), P())
    return jax.shard_map(
        shards,
        mesh=mesh,
        in_specs=placed,
        out_specs=P(("group", "azim"), None, None, None),
        check_vma=False,
    )
```

profile of v0, /device:TPU:1, one launch (start us, length us, event | category | flops | bytes accessed | tf_op | source)
XLA Modules:
  0.0 432.2 jit_solution(5272978858724558747)
XLA Ops:
  0.0 3.9 copy.112
  3.9 7.5 %all-to-all-start = ((bf16[22,64,640]{2,0,1:T(8,128)(2,1)}), bf16[22,64,640]{2,0,1:T(8,128)(2,1)S(1)}, u32[]{:S(2)}, u32[]{:S(2)}) async-start(bf16[22,64,640]{2,0,1:T(8,128)(2,1)} %bitcast.173), calls=%async_computation | async-start | bytes 3932160 | tf_op jit(solution)/shard_map/all_to_all | solution.py:36
  11.4 21.1 %gather_fusion = bf16[64,5,2,20,320]{4,2,3,1,0:T(2,128)(2,1)} fusion(bf16[5,8,2,20,320]{4,2,3,1,0:T(2,128)(2,1)S(1)} %copy-done, s32[1024]{0:T(1024)S(1)} %pad_clamp_fusion), kind=kCustom, calls=%fused_computation | custom fusion | bytes 16384256 | tf_op jit(solution)/shard_map/jit(_take)/gather | solution.py:38
  32.6 18.0 %all-to-all-done = bf16[22,64,640]{2,0,1:T(8,128)(2,1)S(1)} async-done(((bf16[22,64,640]{2,0,1:T(8,128)(2,1)}), bf16[22,64,640]{2,0,1:T(8,128)(2,1)S(1)}, u32[]{:S(2)}, u32[]{:S(2)}) %all-to-all-start) | async-done | bytes 1802272 | tf_op jit(solution)/shard_map/all_to_all | solution.py:36
  50.6 10.5 %all-to-all-start.1 = ((bf16[5,64,2,20,320]{4,2,3,0,1:T(2,128)(2,1)}), bf16[5,64,2,20,320]{4,2,3,0,1:T(2,128)(2,1)}, u32[]{:S(2)}, u32[]{:S(2)}) async-start(bf16[5,64,2,20,320]{4,2,3,0,1:T(2,128)(2,1)} %bitcast.171), calls=%async_computation.1 | async-start | bytes 19660800 | tf_op jit(solution)/shard_map/all_to_all | solution.py:39
  61.1 0.7 copy.125
  62.0 175.3 %all-to-all-done.1 = bf16[5,64,2,20,320]{4,2,3,0,1:T(2,128)(2,1)} async-done(((bf16[5,64,2,20,320]{4,2,3,0,1:T(2,128)(2,1)}), bf16[5,64,2,20,320]{4,2,3,0,1:T(2,128)(2,1)}, u32[]{:S(2)}, u32[]{:S(2)}) %all-to-all-start.1) | async-done | bytes 8192032 | tf_op jit(solution)/shard_map/all_to_all | solution.py:39
  237.3 9.3 %copy.115 = bf16[5,16,4,2,20,320]{5,3,4,1,2,0:T(2,128)(2,1)} copy(bf16[5,16,4,2,20,320]{5,3,4,0,2,1:T(2,128)(2,1)} %bitcast.6) | data formatting | bytes 16384000 | tf_op jit(solution)/shard_map/all_to_all | solution.py:39
  246.5 96.6 %while.15 = (s32[]{:T(128)}, bf16[352,4,640]{2,0,1:T(8,128)(2,1)}, bf16[352,4,640]{2,0,1:T(8,128)(2,1)S(1)}, bf16[16,5]{0,1:T(8,128)(2,1)S(1)}, bf16[5,4,2,320,320]{4,2,3,1,0:T(2,128)(2,1)}, /*index=5*/s32[]{:T(128)}) while((s32[]{:T(128)}, bf16[352,4,640]{2,0,1:T(8,128)(2,1)}, bf16[352,4,640]{2,0,1:T(8,128)(2,1)S(1)}, ...), condition=%wide.region_1.2_spmd.clone.clone, body=%wide.region_0.1_spmd.clone.clone.sunk | while | flops 1674994944 | bytes 79102776 | solution.py:107
  246.7 3.4 constant_dynamic-slice_fusion.4
  250.8 6.1 %maximum_maximum_fusion.2 = bf16[5,640,640]{2,1,0:T(8,128)(2,1)S(1)} fusion(bf16[5,320,320]{2,1,0:T(8,128)(2,1)S(1)} %get-tuple-element.401, bf16[5,320,320]{2,1,0:T(8,128)(2,1)S(1)} %get-tuple-element.402, bf16[5,320,320]{2,1,0:T(8,128)(2,1)S(1)} %fusion.160), kind=kLoop, calls=%fused_computation.7.clone.1 | loop fusion | flops 16384000 | bytes 7168000 | tf_op jit(solution)/shard_map/while/body/eval_jaxpr/concatenate | solution.py:24
  258.8 0.6 convolution_bitcast_fusion.14
  259.4 0.6 convolution_bitcast_fusion.15
  261.7 0.7 fusion.165
  262.3 0.7 convolution_add_fusion.8
  263.0 0.7 convolution_add_fusion.9
  264.1 0.7 convolution_add_fusion.10
  264.8 0.7 convolution_add_fusion.11
  265.5 0.6 fusion.166
  267.7 0.7 convolution_bitcast_fusion.16
  268.4 0.7 convolution_bitcast_fusion.17
  269.7 1.0 fusion.168
  270.8 3.4 constant_dynamic-slice_fusion.4
  274.9 6.1 %maximum_maximum_fusion.2 = bf16[5,640,640]{2,1,0:T(8,128)(2,1)S(1)} fusion(bf16[5,320,320]{2,1,0:T(8,128)(2,1)S(1)} %get-tuple-element.401, bf16[5,320,320]{2,1,0:T(8,128)(2,1)S(1)} %get-tuple-element.402, bf16[5,320,320]{2,1,0:T(8,128)(2,1)S(1)} %fusion.160), kind=kLoop, calls=%fused_computation.7.clone.1 | loop fusion | flops 16384000 | bytes 7168000 | tf_op jit(solution)/shard_map/while/body/eval_jaxpr/concatenate | solution.py:24
  282.9 0.6 convolution_bitcast_fusion.14
  283.5 0.6 convolution_bitcast_fusion.15
  285.8 0.7 fusion.165
  286.5 0.7 convolution_add_fusion.8
  287.2 0.7 convolution_add_fusion.9
  288.3 0.7 convolution_add_fusion.10
  288.9 0.7 convolution_add_fusion.11
  289.6 0.6 fusion.166
  291.9 0.7 convolution_bitcast_fusion.16
  292.6 0.7 convolution_bitcast_fusion.17
  293.9 1.0 fusion.168
  295.0 3.4 constant_dynamic-slice_fusion.4
  299.1 6.1 %maximum_maximum_fusion.2 = bf16[5,640,640]{2,1,0:T(8,128)(2,1)S(1)} fusion(bf16[5,320,320]{2,1,0:T(8,128)(2,1)S(1)} %get-tuple-element.401, bf16[5,320,320]{2,1,0:T(8,128)(2,1)S(1)} %get-tuple-element.402, bf16[5,320,320]{2,1,0:T(8,128)(2,1)S(1)} %fusion.160), kind=kLoop, calls=%fused_computation.7.clone.1 | loop fusion | flops 16384000 | bytes 7168000 | tf_op jit(solution)/shard_map/while/body/eval_jaxpr/concatenate | solution.py:24
  307.1 0.6 convolution_bitcast_fusion.14
  307.7 0.6 convolution_bitcast_fusion.15
  310.0 0.7 fusion.165
  310.6 0.7 convolution_add_fusion.8
  311.3 0.7 convolution_add_fusion.9
  312.4 0.7 convolution_add_fusion.10
  313.1 0.7 convolution_add_fusion.11
  313.8 0.6 fusion.166
  316.0 0.7 convolution_bitcast_fusion.16
  316.7 0.7 convolution_bitcast_fusion.17
  318.0 1.0 fusion.168
  319.1 3.4 constant_dynamic-slice_fusion.4
  323.2 6.1 %maximum_maximum_fusion.2 = bf16[5,640,640]{2,1,0:T(8,128)(2,1)S(1)} fusion(bf16[5,320,320]{2,1,0:T(8,128)(2,1)S(1)} %get-tuple-element.401, bf16[5,320,320]{2,1,0:T(8,128)(2,1)S(1)} %get-tuple-element.402, bf16[5,320,320]{2,1,0:T(8,128)(2,1)S(1)} %fusion.160), kind=kLoop, calls=%fused_computation.7.clone.1 | loop fusion | flops 16384000 | bytes 7168000 | tf_op jit(solution)/shard_map/while/body/eval_jaxpr/concatenate | solution.py:24
  331.2 0.6 convolution_bitcast_fusion.14
  331.8 0.6 convolution_bitcast_fusion.15
  334.1 0.7 fusion.165
  334.8 0.7 convolution_add_fusion.8
  335.5 0.7 convolution_add_fusion.9
  336.6 0.7 convolution_add_fusion.10
  337.2 0.7 convolution_add_fusion.11
  340.2 0.7 convolution_bitcast_fusion.16
  340.9 0.7 convolution_bitcast_fusion.17
  342.2 1.0 fusion.168
  343.1 2.4 copy.118
  345.6 84.3 %all_to_all.51 = bf16[352,4,640]{2,1,0:T(4,128)(2,1)S(1)} all-to-all(bf16[352,4,640]{2,1,0:T(4,128)(2,1)S(1)} %copy.118), channel_id=1, replica_groups=mesh['group'=2,'azim'=16] {'azim'}, dimensions={0} | all-to-all | bytes 3604480 | tf_op jit(solution)/shard_map/all_to_all | solution.py:108
  429.8 0.9 copy.119
  430.7 1.4 reshape.120
  (117 shorter events, 28.5 us)
Async XLA Ops:
  0.0 11.4 %copy-start = (bf16[5,8,2,20,320]{4,2,3,1,0:T(2,128)(2,1)S(1)}, bf16[5,8,2,20,320]{4,2,3,1,0:T(2,128)(2,1)}, u32[]{:S(2)}) copy-start(bf16[5,8,2,20,320]{4,2,3,1,0:T(2,128)(2,1)} %param.7) | copy-start | bytes 3072004
  3.9 7.5 %copy-start.3 = (s32[64]{0:T(128)S(1)}, s32[64]{0:T(128)}, u32[]{:S(2)}) copy-start(s32[64]{0:T(128)} %constant.113) | copy-start | bytes 772
  3.9 46.7 %all-to-all-start = ((bf16[22,64,640]{2,0,1:T(8,128)(2,1)}), bf16[22,64,640]{2,0,1:T(8,128)(2,1)S(1)}, u32[]{:S(2)}, u32[]{:S(2)}) async-start(bf16[22,64,640]{2,0,1:T(8,128)(2,1)} %bitcast.173), calls=%async_computation | async-start | bytes 3932160 | tf_op jit(solution)/shard_map/all_to_all | solution.py:36
  50.6 10.5 %copy-start.2 = (s32[16,5]{0,1:T(8,128)S(1)}, s32[16,5]{0,1:T(8,128)}, u32[]{:S(2)}) copy-start(s32[16,5]{0,1:T(8,128)} %param.8) | copy-start | bytes 964
  50.6 186.7 %all-to-all-start.1 = ((bf16[5,64,2,20,320]{4,2,3,0,1:T(2,128)(2,1)}), bf16[5,64,2,20,320]{4,2,3,0,1:T(2,128)(2,1)}, u32[]{:S(2)}, u32[]{:S(2)}) async-start(bf16[5,64,2,20,320]{4,2,3,0,1:T(2,128)(2,1)} %bitcast.171), calls=%async_computation.1 | async-start | bytes 19660800 | tf_op jit(solution)/shard_map/all_to_all | solution.py:39
  429.8 2.3 copy-start.1
where the time goes:
time: 433 us; the launch traced here: 432 us
  waiting for transfers between devices  193 us (45%)
  blocking collectives  84.3 us (19%)
  local copies, waits for them, and re-layouts  61.2 us (14%)
  other arithmetic  41.7 us (10%)
  matrix products  32.7 us (8%)
  starting transfers between devices  17.9 us (4%)
    all_to_all x1, waiting for transfers between devices, shards(): lax.all_to_all(outgoing, 'azim', split_axis=1, concat_axis=3, tiled=True)  175 us
    all_to_all x1, blocking collectives, shards(): lax.all_to_all(finished, 'azim', split_axis=0, concat_axis=1, tiled=True)  84.3 us
    concatenate x4, other arithmetic, real_form(): return jnp.concatenate([upper, lower], axis=1)  24.3 us
    gather x1, local copies, waits for them, and re-layouts, shards(): outgoing = jnp.take(jacobian, jnp.asarray(targets, dtype=jnp.int32), axis=1)  21.1 us
    all_to_all x1, waiting for transfers between devices, shards(): lax.all_to_all(flattened, 'azim', split_axis=1, concat_axis=0, tiled=True)  18 us
    dynamic_slice x8, local copies, waits for them, and re-layouts, transform(): lax.dynamic_index_in_dim(local_jac, position, 1, keepdims=False)  15 us
    dot_general x20, matrix products, transform(): jnp.einsum('qri,oi->qro', moved, operator[order_idx], preferred_element_t...  13.5 us
    all_to_all x1, starting transfers between devices, shards(): lax.all_to_all(outgoing, 'azim', split_axis=1, concat_axis=3, tiled=True)  10.5 us
  transfers between devices with their start and end apart: 2, of which 2 were waited for; matrix products, arithmetic and copies ran while one was open for 5% of the time, Pallas kernels for 0%

commit v1 on v0

--- a/solution.py
+++ b/solution.py
@@ -6,6 +6,42 @@
 from jax.sharding import PartitionSpec as P
 
 BLADES = 22
+
+
+def launch_regions_up(m, along_dim, t0):
+    oldest = m.shape
+    clean = jnp.moveaxis(
+        m.reshape(*oldest[:along_dim], t0, oldest[along_dim] // t0, *oldest[along_dim + 1 :]),
+        along_dim,
+        0,
+    )
+    return clean
+
+
+def keep_up_area(inp, in_dim):
+    inp = jnp.moveaxis(inp, 0, in_dim)
+    current_arr = inp.shape
+    mid_arr = inp.reshape(
+        *current_arr[:in_dim],
+        current_arr[in_dim] * current_arr[in_dim + 1],
+        *current_arr[in_dim + 2 :]
+    )
+    return mid_arr
+
+
+def produce_streams(raw, lane_axis, local_array, frame):
+    f_now, q_next = (lax.axis_size(lane_axis), lax.axis_index(lane_axis))
+    new = launch_regions_up(raw, local_array, f_now)
+    everything = new
+    for src_i in range(1, f_now):
+        row_out, field_out = ((q_next + src_i) % f_now, (q_next - src_i) % f_now)
+        raw_out = lax.dynamic_index_in_dim(new, row_out, 0)
+        local_out = lax.ppermute(
+            raw_out, lane_axis, perm=list(map(lambda pp: (pp, (pp + src_i) % f_now), range(f_now)))
+        )
+        everything = lax.dynamic_update_slice_in_dim(everything, local_out, field_out, axis=0)
+    vec_out = keep_up_area(everything, frame)
+    return vec_out
 
 
 def twiddles(row_count, col_count, modulus):
@@ -105,7 +141,7 @@
 
     initial = jnp.zeros((stations, per_device, full_width), jnp.bfloat16)
     finished = lax.fori_loop(0, per_device, transform, initial)
-    returned = lax.all_to_all(finished, "azim", split_axis=0, concat_axis=1, tiled=True)
+    returned = produce_streams(finished, "azim", 0, 1)
     return returned.reshape(local_stations, axial_count, freq_count, full_width)
 
 

time: 433 us -> 442 us (1.021)
  blocking collectives: 84.3 us -> 0 us
  starting transfers between devices: 17.9 us -> 98.4 us
  waiting for transfers between devices: 193 us -> 200 us
  local copies, waits for them, and re-layouts: 61.2 us -> 67.2 us
    all_to_all x1 -> x0, blocking collectives: 84.3 us -> none  [shards(): lax.all_to_all(finished, 'azim', split_axis=0, concat_axis=1, tiled=True)]
    ppermute x0 -> x15, starting transfers between devices: none -> 80.4 us  [produce_streams(): lax.ppermute(raw_out, lane_axis, perm=list(map(lambda pp: (pp, (pp + src_...]
    ppermute x0 -> x15, waiting for transfers between devices: none -> 6.58 us  [produce_streams(): lax.ppermute(raw_out, lane_axis, perm=list(map(lambda pp: (pp, (pp + src_...]
  transfers between devices with their start and end apart: 2 -> 17, of which waited for: 2 -> 7; matrix products, arithmetic and copies ran while one was open for 5% -> 5% of each run, Pallas kernels for 0% -> 0%
where the time goes in v1:
time: 442 us; the launch traced here: 441 us
  waiting for transfers between devices  200 us (45%)
  starting transfers between devices  98.4 us (22%)
  local copies, waits for them, and re-layouts  67.2 us (15%)
  other arithmetic  41.7 us (9%)
  matrix products  32.7 us (7%)
    all_to_all x1, waiting for transfers between devices, shards(): lax.all_to_all(outgoing, 'azim', split_axis=1, concat_axis=3, tiled=True)  175 us
    ppermute x15, starting transfers between devices, produce_streams(): lax.ppermute(raw_out, lane_axis, perm=list(map(lambda pp: (pp, (pp + src_...  80.4 us
    concatenate x4, other arithmetic, real_form(): return jnp.concatenate([upper, lower], axis=1)  24.3 us
    gather x1, local copies, waits for them, and re-layouts, shards(): outgoing = jnp.take(jacobian, jnp.asarray(targets, dtype=jnp.int32), axis=1)  21.1 us
    all_to_all x1, waiting for transfers between devices, shards(): lax.all_to_all(flattened, 'azim', split_axis=1, concat_axis=0, tiled=True)  18 us
    dynamic_slice x8, local copies, waits for them, and re-layouts, transform(): lax.dynamic_index_in_dim(local_jac, position, 1, keepdims=False)  15 us
    dot_general x20, matrix products, transform(): jnp.einsum('qri,oi->qro', moved, operator[order_idx], preferred_element_t...  13.5 us
    all_to_all x1, starting transfers between devices, shards(): lax.all_to_all(outgoing, 'azim', split_axis=1, concat_axis=3, tiled=True)  10.5 us
  transfers between devices with their start and end apart: 17, of which 7 were waited for; matrix products, arithmetic and copies ran while one was open for 5% of the time, Pallas kernels for 0%

profile of v1, /device:TPU:1, one launch (start us, length us, event | category | flops | bytes accessed | tf_op | source)
XLA Modules:
  0.0 441.0 jit_solution(17199434742388690631)
XLA Ops:
  0.0 3.9 copy.142
  3.9 7.5 %all-to-all-start = ((bf16[22,64,640]{2,0,1:T(8,128)(2,1)}), bf16[22,64,640]{2,0,1:T(8,128)(2,1)S(1)}, u32[]{:S(2)}, u32[]{:S(2)}) async-start(bf16[22,64,640]{2,0,1:T(8,128)(2,1)} %bitcast.175), calls=%async_computation | async-start | bytes 3932160 | tf_op jit(solution)/shard_map/all_to_all | solution.py:72
  11.4 21.1 %gather_fusion = bf16[64,5,2,20,320]{4,2,3,1,0:T(2,128)(2,1)} fusion(bf16[5,8,2,20,320]{4,2,3,1,0:T(2,128)(2,1)S(1)} %copy-done, s32[1024]{0:T(1024)S(1)} %pad_clamp_fusion), kind=kCustom, calls=%fused_computation | custom fusion | bytes 16384256 | tf_op jit(solution)/shard_map/jit(_take)/gather | solution.py:74
  32.5 18.0 %all-to-all-done = bf16[22,64,640]{2,0,1:T(8,128)(2,1)S(1)} async-done(((bf16[22,64,640]{2,0,1:T(8,128)(2,1)}), bf16[22,64,640]{2,0,1:T(8,128)(2,1)S(1)}, u32[]{:S(2)}, u32[]{:S(2)}) %all-to-all-start) | async-done | bytes 1802272 | tf_op jit(solution)/shard_map/all_to_all | solution.py:72
  50.5 10.5 %all-to-all-start.1 = ((bf16[5,64,2,20,320]{4,2,3,0,1:T(2,128)(2,1)}), bf16[5,64,2,20,320]{4,2,3,0,1:T(2,128)(2,1)}, u32[]{:S(2)}, u32[]{:S(2)}) async-start(bf16[5,64,2,20,320]{4,2,3,0,1:T(2,128)(2,1)} %bitcast.170), calls=%async_computation.1 | async-start | bytes 19660800 | tf_op jit(solution)/shard_map/all_to_all | solution.py:75
  61.1 0.7 copy.155
  62.0 175.2 %all-to-all-done.1 = bf16[5,64,2,20,320]{4,2,3,0,1:T(2,128)(2,1)} async-done(((bf16[5,64,2,20,320]{4,2,3,0,1:T(2,128)(2,1)}), bf16[5,64,2,20,320]{4,2,3,0,1:T(2,128)(2,1)}, u32[]{:S(2)}, u32[]{:S(2)}) %all-to-all-start.1) | async-done | bytes 8192032 | tf_op jit(solution)/shard_map/all_to_all | solution.py:75
  237.2 9.2 %copy.145 = bf16[5,16,4,2,20,320]{5,3,4,1,2,0:T(2,128)(2,1)} copy(bf16[5,16,4,2,20,320]{5,3,4,0,2,1:T(2,128)(2,1)} %bitcast.6) | data formatting | bytes 16384000 | tf_op jit(solution)/shard_map/all_to_all | solution.py:75
  246.5 96.6 %while.15 = (s32[]{:T(128)}, bf16[352,4,640]{2,0,1:T(8,128)(2,1)}, bf16[352,4,640]{2,0,1:T(8,128)(2,1)S(1)}, bf16[16,5]{0,1:T(8,128)(2,1)S(1)}, bf16[5,4,2,320,320]{4,2,3,1,0:T(2,128)(2,1)}, /*index=5*/s32[]{:T(128)}) while((s32[]{:T(128)}, bf16[352,4,640]{2,0,1:T(8,128)(2,1)}, bf16[352,4,640]{2,0,1:T(8,128)(2,1)S(1)}, ...), condition=%wide.region_1.2_spmd.clone.clone, body=%wide.region_0.1_spmd.clone.clone.sunk | while | flops 1674994944 | bytes 79102776 | solution.py:143
  246.6 3.4 constant_dynamic-slice_fusion.19
  250.7 6.1 %maximum_maximum_fusion.2 = bf16[5,640,640]{2,1,0:T(8,128)(2,1)S(1)} fusion(bf16[5,320,320]{2,1,0:T(8,128)(2,1)S(1)} %get-tuple-element.416, bf16[5,320,320]{2,1,0:T(8,128)(2,1)S(1)} %get-tuple-element.417, bf16[5,320,320]{2,1,0:T(8,128)(2,1)S(1)} %fusion.160), kind=kLoop, calls=%fused_computation.7.clone.1 | loop fusion | flops 16384000 | bytes 7168000 | tf_op jit(solution)/shard_map/while/body/eval_jaxpr/concatenate | solution.py:60
  261.6 0.7 fusion.165
  262.3 0.7 convolution_add_fusion.8
  263.0 0.7 convolution_add_fusion.9
  264.1 0.7 convolution_add_fusion.10
  264.7 0.7 convolution_add_fusion.11
  267.7 0.7 convolution_bitcast_fusion.16
  268.4 0.7 convolution_bitcast_fusion.17
  269.7 1.0 fusion.168
  270.8 3.4 constant_dynamic-slice_fusion.19
  274.9 6.1 %maximum_maximum_fusion.2 = bf16[5,640,640]{2,1,0:T(8,128)(2,1)S(1)} fusion(bf16[5,320,320]{2,1,0:T(8,128)(2,1)S(1)} %get-tuple-element.416, bf16[5,320,320]{2,1,0:T(8,128)(2,1)S(1)} %get-tuple-element.417, bf16[5,320,320]{2,1,0:T(8,128)(2,1)S(1)} %fusion.160), kind=kLoop, calls=%fused_computation.7.clone.1 | loop fusion | flops 16384000 | bytes 7168000 | tf_op jit(solution)/shard_map/while/body/eval_jaxpr/concatenate | solution.py:60
  285.8 0.7 fusion.165
  287.1 0.7 convolution_add_fusion.9
  288.9 0.7 convolution_add_fusion.11
  291.8 0.7 convolution_bitcast_fusion.16
  292.5 0.7 convolution_bitcast_fusion.17
  293.8 1.0 fusion.168
  294.9 3.4 constant_dynamic-slice_fusion.19
  299.0 6.1 %maximum_maximum_fusion.2 = bf16[5,640,640]{2,1,0:T(8,128)(2,1)S(1)} fusion(bf16[5,320,320]{2,1,0:T(8,128)(2,1)S(1)} %get-tuple-element.416, bf16[5,320,320]{2,1,0:T(8,128)(2,1)S(1)} %get-tuple-element.417, bf16[5,320,320]{2,1,0:T(8,128)(2,1)S(1)} %fusion.160), kind=kLoop, calls=%fused_computation.7.clone.1 | loop fusion | flops 16384000 | bytes 7168000 | tf_op jit(solution)/shard_map/while/body/eval_jaxpr/concatenate | solution.py:60
  309.9 0.7 fusion.165
  311.3 0.7 convolution_add_fusion.9
  313.0 0.7 convolution_add_fusion.11
  316.0 0.7 convolution_bitcast_fusion.16
  316.7 0.7 convolution_bitcast_fusion.17
  318.0 1.0 fusion.168
  319.1 3.4 constant_dynamic-slice_fusion.19
  323.2 6.1 %maximum_maximum_fusion.2 = bf16[5,640,640]{2,1,0:T(8,128)(2,1)S(1)} fusion(bf16[5,320,320]{2,1,0:T(8,128)(2,1)S(1)} %get-tuple-element.416, bf16[5,320,320]{2,1,0:T(8,128)(2,1)S(1)} %get-tuple-element.417, bf16[5,320,320]{2,1,0:T(8,128)(2,1)S(1)} %fusion.160), kind=kLoop, calls=%fused_computation.7.clone.1 | loop fusion | flops 16384000 | bytes 7168000 | tf_op jit(solution)/shard_map/while/body/eval_jaxpr/concatenate | solution.py:60
  334.1 0.7 fusion.165
  335.4 0.7 convolution_add_fusion.9
  337.2 0.7 convolution_add_fusion.11
  340.1 0.7 convolution_bitcast_fusion.16
  340.8 0.7 convolution_bitcast_fusion.17
  342.1 1.0 fusion.168
  343.1 2.4 copy.148
  345.6 13.2 %collective-permute-start = (bf16[1,22,4,640]{3,2,1,0:T(4,128)(2,1)S(1)}, bf16[1,22,4,640]{3,2,1,0:T(4,128)(2,1)S(1)}, u32[]{:S(2)}, u32[]{:S(2)}) collective-permute-start(bf16[1,22,4,640]{3,2,1,0:T(4,128)(2,1)S(1)} %constant_dynamic-slice_fusion.16), channel_id=1, source_target_pairs={{0,1},{1,2},{2,3},{3,4},{4,5},{5,6},{6,7},{7,8},{8,9},{9,10},{10,1... | collective-permute-start | bytes 337928 | tf_op jit(solution)/shard_map/ppermute | solution.py:39
  358.7 1.8 collective-permute-done
  360.5 1.4 constant_dynamic-slice_fusion.2
  362.0 25.1 %collective-permute-start.1 = (bf16[1,22,4,640]{3,2,1,0:T(4,128)(2,1)S(1)}, bf16[1,22,4,640]{3,2,1,0:T(4,128)(2,1)S(1)}, u32[]{:S(2)}, u32[]{:S(2)}) collective-permute-start(bf16[1,22,4,640]{3,2,1,0:T(4,128)(2,1)S(1)} %get-tuple-element.354), channel_id=1, source_target_pairs={{0,2},{1,3},{2,4},{3,5},{4,6},{5,7},{6,8},{7,9},{8,10},{9,11},{10,... | collective-permute-start | bytes 337928 | tf_op jit(solution)/shard_map/ppermute | solution.py:39
  387.0 4.2 collective-permute-start.2
  391.2 1.0 collective-permute-start.3
  392.2 1.2 collective-permute-start.4
  393.4 1.6 collective-permute-start.5
  395.0 2.6 collective-permute-start.6
  397.7 0.9 collective-permute-done.2
  398.6 1.5 collective-permute-start.7
  400.2 2.7 collective-permute-start.8
  403.0 14.6 %collective-permute-start.9 = (bf16[1,22,4,640]{3,2,1,0:T(4,128)(2,1)S(1)}, bf16[1,22,4,640]{3,2,1,0:T(4,128)(2,1)S(1)}, u32[]{:S(2)}, u32[]{:S(2)}) collective-permute-start(bf16[1,22,4,640]{3,2,1,0:T(4,128)(2,1)S(1)} %get-tuple-element.346), channel_id=1, source_target_pairs={{0,10},{1,11},{2,12},{3,13},{4,14},{5,15},{6,0},{7,1},{8,2},{9,3},... | collective-permute-start | bytes 337928 | tf_op jit(solution)/shard_map/ppermute | solution.py:39
  417.6 4.7 %collective-permute-start.10 = (bf16[1,22,4,640]{3,2,1,0:T(4,128)(2,1)S(1)}, bf16[1,22,4,640]{3,2,1,0:T(4,128)(2,1)S(1)}, u32[]{:S(2)}, u32[]{:S(2)}) collective-permute-start(bf16[1,22,4,640]{3,2,1,0:T(4,128)(2,1)S(1)} %get-tuple-element.345), channel_id=1, source_target_pairs={{0,11},{1,12},{2,13},{3,14},{4,15},{5,0},{6,1},{7,2},{8,3},{9,4},{... | collective-permute-start | bytes 337928 | tf_op jit(solution)/shard_map/ppermute | solution.py:39
  422.4 4.5 %collective-permute-start.11 = (bf16[1,22,4,640]{3,2,1,0:T(4,128)(2,1)S(1)}, bf16[1,22,4,640]{3,2,1,0:T(4,128)(2,1)S(1)}, u32[]{:S(2)}, u32[]{:S(2)}) collective-permute-start(bf16[1,22,4,640]{3,2,1,0:T(4,128)(2,1)S(1)} %get-tuple-element.344), channel_id=1, source_target_pairs={{0,12},{1,13},{2,14},{3,15},{4,0},{5,1},{6,2},{7,3},{8,4},{9,5},{1... | collective-permute-start | bytes 337928 | tf_op jit(solution)/shard_map/ppermute | solution.py:39
  426.9 3.0 collective-permute-start.12
  430.9 1.3 collective-permute-done.12
  432.2 2.4 collective-permute-done.13
  434.9 2.2 copy.149
  437.1 3.9 reshape_reshape.3
  (162 shorter events, 40.9 us)
Async XLA Ops:
  0.0 11.4 %copy-start = (bf16[5,8,2,20,320]{4,2,3,1,0:T(2,128)(2,1)S(1)}, bf16[5,8,2,20,320]{4,2,3,1,0:T(2,128)(2,1)}, u32[]{:S(2)}) copy-start(bf16[5,8,2,20,320]{4,2,3,1,0:T(2,128)(2,1)} %param.7) | copy-start | bytes 3072004
  3.9 7.5 %copy-start.3 = (s32[64]{0:T(128)S(1)}, s32[64]{0:T(128)}, u32[]{:S(2)}) copy-start(s32[64]{0:T(128)} %constant.328) | copy-start | bytes 772
  3.9 46.7 %all-to-all-start = ((bf16[22,64,640]{2,0,1:T(8,128)(2,1)}), bf16[22,64,640]{2,0,1:T(8,128)(2,1)S(1)}, u32[]{:S(2)}, u32[]{:S(2)}) async-start(bf16[22,64,640]{2,0,1:T(8,128)(2,1)} %bitcast.175), calls=%async_computation | async-start | bytes 3932160 | tf_op jit(solution)/shard_map/all_to_all | solution.py:72
  50.5 10.5 %copy-start.2 = (s32[16,5]{0,1:T(8,128)S(1)}, s32[16,5]{0,1:T(8,128)}, u32[]{:S(2)}) copy-start(s32[16,5]{0,1:T(8,128)} %param.8) | copy-start | bytes 964
  50.5 186.7 %all-to-all-start.1 = ((bf16[5,64,2,20,320]{4,2,3,0,1:T(2,128)(2,1)}), bf16[5,64,2,20,320]{4,2,3,0,1:T(2,128)(2,1)}, u32[]{:S(2)}, u32[]{:S(2)}) async-start(bf16[5,64,2,20,320]{4,2,3,0,1:T(2,128)(2,1)} %bitcast.170), calls=%async_computation.1 | async-start | bytes 19660800 | tf_op jit(solution)/shard_map/all_to_all | solution.py:75
  345.6 14.9 %collective-permute-start = (bf16[1,22,4,640]{3,2,1,0:T(4,128)(2,1)S(1)}, bf16[1,22,4,640]{3,2,1,0:T(4,128)(2,1)S(1)}, u32[]{:S(2)}, u32[]{:S(2)}) collective-permute-start(bf16[1,22,4,640]{3,2,1,0:T(4,128)(2,1)S(1)} %constant_dynamic-slice_fusion.16), channel_id=1, source_target_pairs={{0,1},{1,2},{2,3},{3,4},{4,5},{5,6},{6,7},{7,8},{8,9},{9,10},{10,1... | collective-permute-start | bytes 337928 | tf_op jit(solution)/shard_map/ppermute | solution.py:39
  362.0 33.0 %collective-permute-start.1 = (bf16[1,22,4,640]{3,2,1,0:T(4,128)(2,1)S(1)}, bf16[1,22,4,640]{3,2,1,0:T(4,128)(2,1)S(1)}, u32[]{:S(2)}, u32[]{:S(2)}) collective-permute-start(bf16[1,22,4,640]{3,2,1,0:T(4,128)(2,1)S(1)} %get-tuple-element.354), channel_id=1, source_target_pairs={{0,2},{1,3},{2,4},{3,5},{4,6},{5,7},{6,8},{7,9},{8,10},{9,11},{10,... | collective-permute-start | bytes 337928 | tf_op jit(solution)/shard_map/ppermute | solution.py:39
  387.0 11.6 %collective-permute-start.2 = (bf16[1,22,4,640]{3,2,1,0:T(4,128)(2,1)S(1)}, bf16[1,22,4,640]{3,2,1,0:T(4,128)(2,1)S(1)}, u32[]{:S(2)}, u32[]{:S(2)}) collective-permute-start(bf16[1,22,4,640]{3,2,1,0:T(4,128)(2,1)S(1)} %get-tuple-element.353), channel_id=1, source_target_pairs={{0,3},{1,4},{2,5},{3,6},{4,7},{5,8},{6,9},{7,10},{8,11},{9,12},{10... | collective-permute-start | bytes 337928 | tf_op jit(solution)/shard_map/ppermute | solution.py:39
  391.2 9.0 %collective-permute-start.3 = (bf16[1,22,4,640]{3,2,1,0:T(4,128)(2,1)}, bf16[1,22,4,640]{3,2,1,0:T(4,128)(2,1)S(1)}, u32[]{:S(2)}, u32[]{:S(2)}) collective-permute-start(bf16[1,22,4,640]{3,2,1,0:T(4,128)(2,1)} %get-tuple-element.352), channel_id=1, source_target_pairs={{0,4},{1,5},{2,6},{3,7},{4,8},{5,9},{6,10},{7,11},{8,12},{9,13},{1... | collective-permute-start | bytes 337928 | tf_op jit(solution)/shard_map/ppermute | solution.py:39
  392.2 10.7 %collective-permute-start.4 = (bf16[1,22,4,640]{3,2,1,0:T(4,128)(2,1)}, bf16[1,22,4,640]{3,2,1,0:T(4,128)(2,1)S(1)}, u32[]{:S(2)}, u32[]{:S(2)}) collective-permute-start(bf16[1,22,4,640]{3,2,1,0:T(4,128)(2,1)} %get-tuple-element.351), channel_id=1, source_target_pairs={{0,5},{1,6},{2,7},{3,8},{4,9},{5,10},{6,11},{7,12},{8,13},{9,14},{... | collective-permute-start | bytes 337928 | tf_op jit(solution)/shard_map/ppermute | solution.py:39
  393.4 24.2 %collective-permute-start.5 = (bf16[1,22,4,640]{3,2,1,0:T(4,128)(2,1)}, bf16[1,22,4,640]{3,2,1,0:T(4,128)(2,1)S(1)}, u32[]{:S(2)}, u32[]{:S(2)}) collective-permute-start(bf16[1,22,4,640]{3,2,1,0:T(4,128)(2,1)} %get-tuple-element.350), channel_id=1, source_target_pairs={{0,6},{1,7},{2,8},{3,9},{4,10},{5,11},{6,12},{7,13},{8,14},{9,15},... | collective-permute-start | bytes 337928 | tf_op jit(solution)/shard_map/ppermute | solution.py:39
  395.0 27.4 %collective-permute-start.6 = (bf16[1,22,4,640]{3,2,1,0:T(4,128)(2,1)}, bf16[1,22,4,640]{3,2,1,0:T(4,128)(2,1)S(1)}, u32[]{:S(2)}, u32[]{:S(2)}) collective-permute-start(bf16[1,22,4,640]{3,2,1,0:T(4,128)(2,1)} %get-tuple-element.349), channel_id=1, source_target_pairs={{0,7},{1,8},{2,9},{3,10},{4,11},{5,12},{6,13},{7,14},{8,15},{9,0},... | collective-permute-start | bytes 337928 | tf_op jit(solution)/shard_map/ppermute | solution.py:39
  398.6 28.3 %collective-permute-start.7 = (bf16[1,22,4,640]{3,2,1,0:T(4,128)(2,1)}, bf16[1,22,4,640]{3,2,1,0:T(4,128)(2,1)S(1)}, u32[]{:S(2)}, u32[]{:S(2)}) collective-permute-start(bf16[1,22,4,640]{3,2,1,0:T(4,128)(2,1)} %get-tuple-element.348), channel_id=1, source_target_pairs={{0,8},{1,9},{2,10},{3,11},{4,12},{5,13},{6,14},{7,15},{8,0},{9,1},... | collective-permute-start | bytes 337928 | tf_op jit(solution)/shard_map/ppermute | solution.py:39
  400.2 29.7 %collective-permute-start.8 = (bf16[1,22,4,640]{3,2,1,0:T(4,128)(2,1)S(1)}, bf16[1,22,4,640]{3,2,1,0:T(4,128)(2,1)S(1)}, u32[]{:S(2)}, u32[]{:S(2)}) collective-permute-start(bf16[1,22,4,640]{3,2,1,0:T(4,128)(2,1)S(1)} %get-tuple-element.347), channel_id=1, source_target_pairs={{0,9},{1,10},{2,11},{3,12},{4,13},{5,14},{6,15},{7,0},{8,1},{9,2},... | collective-permute-start | bytes 337928 | tf_op jit(solution)/shard_map/ppermute | solution.py:39
  403.0 27.6 %collective-permute-start.9 = (bf16[1,22,4,640]{3,2,1,0:T(4,128)(2,1)S(1)}, bf16[1,22,4,640]{3,2,1,0:T(4,128)(2,1)S(1)}, u32[]{:S(2)}, u32[]{:S(2)}) collective-permute-start(bf16[1,22,4,640]{3,2,1,0:T(4,128)(2,1)S(1)} %get-tuple-element.346), channel_id=1, source_target_pairs={{0,10},{1,11},{2,12},{3,13},{4,14},{5,15},{6,0},{7,1},{8,2},{9,3},... | collective-permute-start | bytes 337928 | tf_op jit(solution)/shard_map/ppermute | solution.py:39
  417.6 13.1 %collective-permute-start.10 = (bf16[1,22,4,640]{3,2,1,0:T(4,128)(2,1)S(1)}, bf16[1,22,4,640]{3,2,1,0:T(4,128)(2,1)S(1)}, u32[]{:S(2)}, u32[]{:S(2)}) collective-permute-start(bf16[1,22,4,640]{3,2,1,0:T(4,128)(2,1)S(1)} %get-tuple-element.345), channel_id=1, source_target_pairs={{0,11},{1,12},{2,13},{3,14},{4,15},{5,0},{6,1},{7,2},{8,3},{9,4},{... | collective-permute-start | bytes 337928 | tf_op jit(solution)/shard_map/ppermute | solution.py:39
  422.4 8.4 %collective-permute-start.11 = (bf16[1,22,4,640]{3,2,1,0:T(4,128)(2,1)S(1)}, bf16[1,22,4,640]{3,2,1,0:T(4,128)(2,1)S(1)}, u32[]{:S(2)}, u32[]{:S(2)}) collective-permute-start(bf16[1,22,4,640]{3,2,1,0:T(4,128)(2,1)S(1)} %get-tuple-element.344), channel_id=1, source_target_pairs={{0,12},{1,13},{2,14},{3,15},{4,0},{5,1},{6,2},{7,3},{8,4},{9,5},{1... | collective-permute-start | bytes 337928 | tf_op jit(solution)/shard_map/ppermute | solution.py:39
  426.9 5.2 %collective-permute-start.12 = (bf16[1,22,4,640]{3,2,1,0:T(4,128)(2,1)S(1)}, bf16[1,22,4,640]{3,2,1,0:T(4,128)(2,1)S(1)}, u32[]{:S(2)}, u32[]{:S(2)}) collective-permute-start(bf16[1,22,4,640]{3,2,1,0:T(4,128)(2,1)S(1)} %get-tuple-element.343), channel_id=1, source_target_pairs={{0,13},{1,14},{2,15},{3,0},{4,1},{5,2},{6,3},{7,4},{8,5},{9,6},{10... | collective-permute-start | bytes 337928 | tf_op jit(solution)/shard_map/ppermute | solution.py:39
  430.0 4.6 %collective-permute-start.13 = (bf16[1,22,4,640]{3,2,1,0:T(4,128)(2,1)S(1)}, bf16[1,22,4,640]{3,2,1,0:T(4,128)(2,1)S(1)}, u32[]{:S(2)}, u32[]{:S(2)}) collective-permute-start(bf16[1,22,4,640]{3,2,1,0:T(4,128)(2,1)S(1)} %get-tuple-element.342), channel_id=1, source_target_pairs={{0,14},{1,15},{2,0},{3,1},{4,2},{5,3},{6,4},{7,5},{8,6},{9,7},{10,... | collective-permute-start | bytes 337928 | tf_op jit(solution)/shard_map/ppermute | solution.py:39
  430.6 4.2 collective-permute-start.14
  434.9 6.1 %copy-start.1 = (bf16[5,8,2,20,320]{4,2,3,1,0:T(2,128)(2,1)S(1)}, bf16[5,8,2,20,320]{4,2,3,1,0:T(2,128)(2,1)}, u32[]{:S(2)}) copy-start(bf16[5,8,2,20,320]{4,2,3,1,0:T(2,128)(2,1)} %param.7) | copy-start | bytes 3072004
